TPU v7x, 32 devices: a whole 2x2x4 slice. The times are simulated.
32 devices in a mesh: row: 8 (over z, core), col: 4 (over y, x).
Axes of the slice: x: 2, y: 2, z: 4, core: 2. Of those that a mesh axis runs over, the one named last changes fastest.
Arguments:
- rhs: bfloat16 [3, 8, 64, 256], P(None, 'row'), may hold values from -6 to 6
- dinv: bfloat16 [3, 8, 256, 256], P(None, 'row'), as said below
- tiles: bfloat16 [2, 8, 8, 256, 256], P(None, 'row', 'col'), may hold values from -0.09375 to 0.09375
- pattern: int32 [2, 2, 8, 8], P(None, None, 'row', 'col'), may hold values from 0 to 7, as said below
Outputs:
- solution: float32 [3, 8, 64, 256], P(None, 'row')
Inputs may be any that keep to these rules, and one draw needn't show every extreme that they name: pattern[0, l, p, t] = p; pattern[1, l, p, t] = j has (j) modulo the size of col equal to t // 2; positions may repeat, and repeated tiles add. `dinv`: lower triangular with a positive diagonal.
All inputs are finite; a program needn't handle non-finite values.
Results may differ from a plain program's by a relative error of at most 0.0055.
Values may be sent and summed in bfloat16 or wider, within the bound.
No kernel may reach another device: no remote copies, remote signals or barrier semaphores. Data moves between devices by JAX's collectives and lax.ppermute only.
A program may use at most 64 MiB of HBM per device.

v0:
```python
import jax
import jax.numpy as jnp
from jax import lax
from jax.sharding import PartitionSpec as P


def broadcast(block, axis, holder):
    block = jnp.where(lax.axis_index(axis) == holder, block, jnp.zeros_like(block))
    return lax.psum(block, axis)


def collect(rounded, mine_col, col_count, repeat):
    whole_level = lax.all_gather(rounded, "row", axis=0, tiled=True)
    shaped = whole_level.reshape((repeat, col_count) + rounded.shape)
    picked = lax.dynamic_index_in_dim(shaped, mine_col, 1, keepdims=False)
    return picked.reshape((-1,) + rounded.shape[1:])


def per_device(rhs, dinv, tiles, pattern):
    blocks = rhs.shape[1]
    levels_all = rhs.shape[0]
    col_count = lax.axis_size("col")
    row_count = lax.axis_size("row")
    repeat = row_count // col_count
    mine_row = lax.axis_index("row")
    mine_col = lax.axis_index("col")
    targets = pattern[0, :, 0, :] % blocks
    raw_cols = pattern[1, :, 0, :]
    sources = raw_cols // blocks // col_count * blocks + raw_cols % blocks
    row_pick = (targets[:, None, :] == jnp.arange(blocks, dtype=jnp.int32)[None, :, None]).astype(
        jnp.float32
    )
    col_pick = (
        sources[:, None, :] == jnp.arange(repeat * blocks, dtype=jnp.int32)[None, :, None]
    ).astype(jnp.float32)
    fronts = [rhs]
    forward_all = [[] for front in fronts]
    rounded_all = [None for front in fronts]
    for level_now in range(levels_all):
        front_index = 0
        front_level = fronts[front_index][level_now]
        current = front_level.astype(jnp.float32)
        if level_now > 0:
            nearby = collect(rounded_all[front_index], mine_col, col_count, repeat)
            source = jnp.take(nearby, sources[level_now - 1], axis=0)
            product = jnp.einsum(
                "sjb,sab->sja", source, tiles[level_now - 1, 0], preferred_element_type=jnp.float32
            )
            partial_value = jnp.sum(
                row_pick[level_now - 1][:, :, None, None] * product[None], axis=1
            )
            total_sum = lax.psum(partial_value, "col")
            current = current - total_sum
        solved = jnp.einsum(
            "rjb,rab->rja",
            current.astype(jnp.bfloat16),
            dinv[level_now],
            preferred_element_type=jnp.float32,
        )
        forward_all[front_index].append(solved)
        rounded_all[front_index] = solved.astype(jnp.bfloat16)
    backward_all = [[None] * levels_all for front in fronts]
    following_all = [None for front in fronts]
    for level_now in range(levels_all - 1, -1, -1):
        front_index = 0
        remainder = forward_all[front_index][level_now]
        if level_now < levels_all - 1:
            source = jnp.take(following_all[front_index], targets[level_now], axis=0)
            product = jnp.einsum(
                "sja,sab->sjb", source, tiles[level_now, 0], preferred_element_type=jnp.float32
            )
            partial_value = jnp.sum(col_pick[level_now][:, :, None, None] * product[None], axis=1)
            column_total = lax.psum(partial_value, "row")
            shaped = column_total.reshape((repeat, blocks) + column_total.shape[1:])
            picked = lax.dynamic_index_in_dim(shaped, mine_row // col_count, 0, keepdims=False)
            arrived = broadcast(picked, "col", mine_row % col_count)
            remainder = remainder - arrived
        solved = jnp.einsum(
            "rjb,rba->rja",
            remainder.astype(jnp.bfloat16),
            dinv[level_now],
            preferred_element_type=jnp.float32,
        )
        backward_all[front_index][level_now] = solved
        following_all[front_index] = solved.astype(jnp.bfloat16)
    front_index = 0
    levels_stack = jnp.stack(backward_all[front_index])
    return levels_stack


def solution(mesh):
    in_specs = (
        P(None, "row", None, None),
        P(None, "row", None, None),
        P(None, "row", "col", None, None),
        P(None, None, "row", "col"),
    )
    out_specs = P(None, "row", None, None)
    return jax.shard_map(
        per_device, mesh=mesh, in_specs=in_specs, out_specs=out_specs, check_vma=False
    )
```

profile of v0, /device:TPU:0, one launch (start us, length us, event | category | flops | bytes accessed | tf_op | source)
XLA Modules:
  0.0 337.1 jit_solution(15482950410898514648)
XLA Ops:
  6.5 0.0 copy-start.1
  6.5 0.0 all-reduce.7.cloned.1.call-start
  6.5 1.1 fusion.57
  7.7 0.0 slice-start
  7.7 15.9 %all-gather = bf16[512,256]{1,0:T(8,128)(2,1)S(1)} all-gather(bf16[64,256]{1,0:T(8,128)(2,1)S(1)} %get-tuple-element.15), channel_id=2, replica_groups=mesh['row'=8,'col'=4] {'row'}, dimensions={0}, use_global_device_ids=true | all-gather | bytes 294912 | tf_op jit(solution)/shard_map/all_gather | solution.py:13
  23.6 0.0 copy-start
  23.6 0.0 slice-done
  23.7 0.6 gather_fusion
  24.3 0.0 copy-done.1
  24.3 0.0 copy-start.2
  24.3 0.8 convolution_bitcast_fusion.2
  25.1 0.0 all-reduce.7.cloned.1.call-update
  25.1 0.0 all-reduce.9.cloned.1.call-start
  25.2 43.0 %all-reduce.7.cloned.1.call-done = f32[1,64,256]{2,1,0:T(8,128)} async-done(((f32[1,64,256]{2,1,0:T(8,128)}), f32[1,64,256]{2,1,0:T(8,128)}) %all-reduce.7.cloned.1.call-update) | async-done | bytes 65552 | tf_op jit(solution)/shard_map/psum | solution.py:52
  68.2 0.0 copy-done
  68.2 0.0 copy-done.2
  68.2 1.0 fusion.58
  69.2 14.3 %all-gather.1 = bf16[512,256]{1,0:T(8,128)(2,1)S(1)} all-gather(bf16[64,256]{1,0:T(8,128)(2,1)S(1)} %get-tuple-element.17), channel_id=3, replica_groups=mesh['row'=8,'col'=4] {'row'}, dimensions={0}, use_global_device_ids=true | all-gather | bytes 294912 | tf_op jit(solution)/shard_map/all_gather | solution.py:13
  83.5 0.5 gather_fusion.1
  84.0 0.8 convolution_bitcast_fusion.1
  84.9 0.0 all-reduce.9.cloned.1.call-update
  84.9 0.0 all-reduce.11.cloned.1.call-start
  84.9 41.9 %all-reduce.9.cloned.1.call-done = f32[1,64,256]{2,1,0:T(8,128)} async-done(((f32[1,64,256]{2,1,0:T(8,128)}), f32[1,64,256]{2,1,0:T(8,128)}) %all-reduce.9.cloned.1.call-update) | async-done | bytes 65552 | tf_op jit(solution)/shard_map/psum | solution.py:52
  126.9 1.1 fusion.59
  128.0 0.2 fusion.1
  128.2 0.8 multiply_reduce_fusion.1
  128.9 0.0 all-reduce.11.cloned.1.call-update
  128.9 0.0 all-reduce.13.cloned.1.call-start
  129.0 55.1 %all-reduce.11.cloned.1.call-done = f32[2,64,256]{2,1,0:T(8,128)} async-done(((f32[2,64,256]{2,1,0:T(8,128)}), f32[2,64,256]{2,1,0:T(8,128)}) %all-reduce.11.cloned.1.call-update) | async-done | bytes 131088 | tf_op jit(solution)/shard_map/psum | solution.py:73
  184.1 1.5 dynamic-slice_select_fusion.1
  185.6 0.0 all-reduce.13.cloned.1.call-update
  185.6 0.0 all-reduce.15.cloned.1.call-start
  185.7 42.1 %all-reduce.13.cloned.1.call-done = f32[1,64,256]{2,1,0:T(8,128)} async-done(((f32[1,64,256]{2,1,0:T(8,128)}), f32[1,64,256]{2,1,0:T(8,128)}) %all-reduce.13.cloned.1.call-update) | async-done | bytes 65552 | tf_op jit(solution)/shard_map/psum | solution.py:9
  227.8 1.0 fusion.64
  228.8 0.2 fusion.4
  228.9 0.7 multiply_reduce_fusion
  229.7 0.0 all-reduce.15.cloned.1.call-update
  229.7 0.0 all-reduce.17.cloned.1.call-start
  229.8 55.1 %all-reduce.15.cloned.1.call-done = f32[2,64,256]{2,1,0:T(8,128)} async-done(((f32[2,64,256]{2,1,0:T(8,128)}), f32[2,64,256]{2,1,0:T(8,128)}) %all-reduce.15.cloned.1.call-update) | async-done | bytes 131088 | tf_op jit(solution)/shard_map/psum | solution.py:73
  284.9 1.5 dynamic-slice_select_fusion
  286.4 0.0 all-reduce.17.cloned.1.call-update
  286.4 42.2 %all-reduce.17.cloned.1.call-done = f32[1,64,256]{2,1,0:T(8,128)} async-done(((f32[1,64,256]{2,1,0:T(8,128)}), f32[1,64,256]{2,1,0:T(8,128)}) %all-reduce.17.cloned.1.call-update) | async-done | bytes 65552 | tf_op jit(solution)/shard_map/psum | solution.py:9
  328.5 1.0 convolution_bitcast_fusion
  329.5 0.7 pad_maximum_fusion
  (8 shorter events, 0.1 us)
Async XLA Ops:
  6.5 17.7 %copy-start.1 = (bf16[2,1,2,256,256]{4,3,2,1,0:T(8,128)(2,1)S(1)}, bf16[2,1,2,256,256]{4,3,2,1,0:T(8,128)(2,1)}, u32[]{:S(2)}) copy-start(bf16[2,1,2,256,256]{4,3,2,1,0:T(8,128)(2,1)} %param.10) | copy-start | bytes 1572868
  6.5 61.6 %all-reduce.7.cloned.1.call-start = ((), (), s32[]{:S(2)}) async-start(), calls=%async_computation | async-start | bytes 131072 | tf_op jit(solution)/shard_map/psum | solution.py:52
  7.7 16.0 %slice-start = ((s32[2,2,1,2]{3,2,1,0:T(1,128)}), s32[1,2,1,2]{3,2,1,0:T(1,128)S(1)}, s32[]{:S(2)}) async-start(s32[2,2,1,2]{3,2,1,0:T(1,128)} %param.11), calls=%async_computation.6 | async-start | bytes 2048 | tf_op jit(solution)/shard_map/slice | solution.py:28
  23.6 44.5 %copy-start = (bf16[3,1,256,256]{3,2,1,0:T(8,128)(2,1)S(1)}, bf16[3,1,256,256]{3,2,1,0:T(8,128)(2,1)}, u32[]{:S(2)}) copy-start(bf16[3,1,256,256]{3,2,1,0:T(8,128)(2,1)} %param.9) | copy-start | bytes 1179652
  24.3 43.9 %copy-start.2 = (bf16[3,1,64,256]{3,2,1,0:T(8,128)(2,1)S(1)}, bf16[3,1,64,256]{3,2,1,0:T(8,128)(2,1)}, u32[]{:S(2)}) copy-start(bf16[3,1,64,256]{3,2,1,0:T(8,128)(2,1)} %param.8) | copy-start | bytes 294916
  25.1 101.7 %all-reduce.9.cloned.1.call-start = ((), (), s32[]{:S(2)}) async-start(), calls=%async_computation.1 | async-start | bytes 131072 | tf_op jit(solution)/shard_map/psum | solution.py:52
  84.9 99.2 %all-reduce.11.cloned.1.call-start = ((), (), s32[]{:S(2)}) async-start(), calls=%async_computation.2 | async-start | bytes 262144 | tf_op jit(solution)/shard_map/psum | solution.py:73
  128.9 98.8 %all-reduce.13.cloned.1.call-start = ((), (), s32[]{:S(2)}) async-start(), calls=%async_computation.3 | async-start | bytes 131072 | tf_op jit(solution)/shard_map/psum | solution.py:9
  185.6 99.3 %all-reduce.15.cloned.1.call-start = ((), (), s32[]{:S(2)}) async-start(), calls=%async_computation.4 | async-start | bytes 262144 | tf_op jit(solution)/shard_map/psum | solution.py:73
  229.7 98.8 %all-reduce.17.cloned.1.call-start = ((), (), s32[]{:S(2)}) async-start(), calls=%async_computation.5 | async-start | bytes 131072 | tf_op jit(solution)/shard_map/psum | solution.py:9
Sparse Core Ops, SparseCore 0:
  25.3 42.8 all-reduce.6
  85.0 41.7 all-reduce.8
  129.2 54.9 all-reduce.10
  186.8 40.8 all-reduce.12
  229.9 54.9 all-reduce.14
  287.6 40.8 all-reduce.16
where the time goes:
time: 337 us
  waiting for transfers between devices  279 us (83%)
  blocking collectives  30.2 us (9%)
  between operations  13.6 us (4%)
  matrix products  7.25 us (2%)
  other arithmetic  5.19 us (2%)
    psum x2, waiting for transfers between devices, per_device(): column_total = lax.psum(partial_value, 'row')  110 us
    psum x2, waiting for transfers between devices, per_device(): total_sum = lax.psum(partial_value, 'col')  84.9 us
    psum x2, waiting for transfers between devices, broadcast(): return lax.psum(block, axis)  84.3 us
    all_gather x2, blocking collectives, collect(): whole_level = lax.all_gather(rounded, 'row', axis=0, tiled=True)  30.2 us
  transfers between devices with their start and end apart: 6, of which 6 were waited for; matrix products, arithmetic and copies ran while one was open for 0% of the time, Pallas kernels for 0%

commit v1 on v0

--- a/solution.py
+++ b/solution.py
@@ -70,7 +70,13 @@
                 "sja,sab->sjb", source, tiles[level_now, 0], preferred_element_type=jnp.float32
             )
             partial_value = jnp.sum(col_pick[level_now][:, :, None, None] * product[None], axis=1)
-            column_total = lax.psum(partial_value, "row")
+            shares = lax.psum(1, axis_name="row")
+            column_total = partial_value
+            for t in [rr for rr in (1, 2, 4, 8, 16) if rr < shares]:
+                row_list = []
+                for q in tuple(range(shares)):
+                    row_list.append((q, q ^ t))
+                column_total = column_total + lax.ppermute(column_total, "row", perm=row_list)
             shaped = column_total.reshape((repeat, blocks) + column_total.shape[1:])
             picked = lax.dynamic_index_in_dim(shaped, mine_row // col_count, 0, keepdims=False)
             arrived = broadcast(picked, "col", mine_row % col_count)

time: 337 us -> 255 us (0.76)
  waiting for transfers between devices: 279 us -> 192 us
  starting transfers between devices: 0.21 us -> 8.32 us
    psum x2 -> x0, waiting for transfers between devices: 110 us -> none  [per_device(): column_total = lax.psum(partial_value, 'row')]
    ppermute x0 -> x6, waiting for transfers between devices: none -> 22.8 us  [per_device(): lax.ppermute(column_total, 'row', perm=row_list)]
    ppermute x0 -> x6, starting transfers between devices: none -> 8.19 us  [per_device(): lax.ppermute(column_total, 'row', perm=row_list)]
  transfers between devices with their start and end apart: 6 -> 10, of which waited for: 6 -> 10; matrix products, arithmetic and copies ran while one was open for 0% -> 0% of each run, Pallas kernels for 0% -> 0%
where the time goes in v1:
time: 255 us
  waiting for transfers between devices  192 us (75%)
  blocking collectives  30.2 us (12%)
  between operations  13.3 us (5%)
  starting transfers between devices  8.32 us (3%)
  matrix products  7.2 us (3%)
    psum x2, waiting for transfers between devices, per_device(): total_sum = lax.psum(partial_value, 'col')  84.9 us
    psum x2, waiting for transfers between devices, broadcast(): return lax.psum(block, axis)  83.9 us
    all_gather x2, blocking collectives, collect(): whole_level = lax.all_gather(rounded, 'row', axis=0, tiled=True)  30.2 us
    ppermute x6, waiting for transfers between devices, per_device(): lax.ppermute(column_total, 'row', perm=row_list)  22.8 us
    ppermute x6, starting transfers between devices, per_device(): lax.ppermute(column_total, 'row', perm=row_list)  8.19 us
  transfers between devices with their start and end apart: 10, of which 10 were waited for; matrix products, arithmetic and copies ran while one was open for 0% of the time, Pallas kernels for 0%

profile of v1, /device:TPU:0, one launch (start us, length us, event | category | flops | bytes accessed | tf_op | source)
XLA Modules:
  0.0 254.7 jit_solution(6252298760742957231)
XLA Ops:
  6.5 0.0 copy-start.1
  6.5 0.0 all-reduce.5.cloned.1.call-start
  6.5 0.7 slice.51
  7.3 1.1 fusion.59
  8.4 15.9 %all-gather = bf16[512,256]{1,0:T(8,128)(2,1)S(1)} all-gather(bf16[64,256]{1,0:T(8,128)(2,1)S(1)} %get-tuple-element.15), channel_id=2, replica_groups=mesh['row'=8,'col'=4] {'row'}, dimensions={0}, use_global_device_ids=true | all-gather | bytes 294912 | tf_op jit(solution)/shard_map/all_gather | solution.py:13
  24.3 0.0 copy-start
  24.3 0.5 gather_fusion
  24.9 0.0 copy-done.1
  24.9 0.0 copy-start.2
  24.9 0.8 convolution_bitcast_fusion.2
  25.8 0.0 all-reduce.5.cloned.1.call-update
  25.8 0.0 all-reduce.7.cloned.1.call-start
  25.9 42.9 %all-reduce.5.cloned.1.call-done = f32[1,64,256]{2,1,0:T(8,128)} async-done(((f32[1,64,256]{2,1,0:T(8,128)}), f32[1,64,256]{2,1,0:T(8,128)}) %all-reduce.5.cloned.1.call-update) | async-done | bytes 65552 | tf_op jit(solution)/shard_map/psum | solution.py:52
  68.8 0.0 copy-done
  68.8 0.0 copy-done.2
  68.8 1.0 fusion.60
  69.8 14.3 %all-gather.1 = bf16[512,256]{1,0:T(8,128)(2,1)S(1)} all-gather(bf16[64,256]{1,0:T(8,128)(2,1)S(1)} %get-tuple-element.17), channel_id=3, replica_groups=mesh['row'=8,'col'=4] {'row'}, dimensions={0}, use_global_device_ids=true | all-gather | bytes 294912 | tf_op jit(solution)/shard_map/all_gather | solution.py:13
  84.1 0.5 gather_fusion.1
  84.7 0.8 convolution_bitcast_fusion.1
  85.5 0.0 all-reduce.7.cloned.1.call-update
  85.5 0.0 all-reduce.9.cloned.1.call-start
  85.6 41.9 %all-reduce.7.cloned.1.call-done = f32[1,64,256]{2,1,0:T(8,128)} async-done(((f32[1,64,256]{2,1,0:T(8,128)}), f32[1,64,256]{2,1,0:T(8,128)}) %all-reduce.7.cloned.1.call-update) | async-done | bytes 65552 | tf_op jit(solution)/shard_map/psum | solution.py:52
  127.5 1.1 fusion.61
  128.6 0.2 fusion.1
  128.8 0.1 multiply_reduce_fusion.1
  128.9 0.1 collective-permute-start
  129.0 1.3 collective-permute-done
  130.3 1.6 collective-permute-start.1
  131.9 4.1 %collective-permute-done.1 = f32[2,64,256]{2,1,0:T(8,128)S(1)} collective-permute-done((f32[2,64,256]{2,1,0:T(8,128)S(1)}, f32[2,64,256]{2,1,0:T(8,128)S(1)}, u32[]{:S(2)}, u32[]{:S(2)}) %collective-permute-start.1) | collective-permute-done | bytes 131104 | tf_op jit(solution)/shard_map/ppermute | solution.py:79
  136.0 2.5 collective-permute-start.2
  138.5 6.0 %collective-permute-done.2 = f32[2,64,256]{2,1,0:T(8,128)S(1)} collective-permute-done((f32[2,64,256]{2,1,0:T(8,128)S(1)}, f32[2,64,256]{2,1,0:T(8,128)S(1)}, u32[]{:S(2)}, u32[]{:S(2)}) %collective-permute-start.2) | collective-permute-done | bytes 131104 | tf_op jit(solution)/shard_map/ppermute | solution.py:79
  144.4 0.6 fusion.27
  145.1 0.0 all-reduce.9.cloned.1.call-update
  145.1 0.0 all-reduce.11.cloned.1.call-start
  145.2 41.9 %all-reduce.9.cloned.1.call-done = f32[1,64,256]{2,1,0:T(8,128)} async-done(((f32[1,64,256]{2,1,0:T(8,128)}), f32[1,64,256]{2,1,0:T(8,128)}) %all-reduce.9.cloned.1.call-update) | async-done | bytes 65552 | tf_op jit(solution)/shard_map/psum | solution.py:9
  187.1 1.0 fusion.66
  188.0 0.2 fusion.4
  188.2 0.1 multiply_reduce_fusion
  188.3 0.1 collective-permute-start.3
  188.4 1.3 collective-permute-done.3
  189.8 1.6 collective-permute-start.4
  191.3 4.1 %collective-permute-done.4 = f32[2,64,256]{2,1,0:T(8,128)S(1)} collective-permute-done((f32[2,64,256]{2,1,0:T(8,128)S(1)}, f32[2,64,256]{2,1,0:T(8,128)S(1)}, u32[]{:S(2)}, u32[]{:S(2)}) %collective-permute-start.4) | collective-permute-done | bytes 131104 | tf_op jit(solution)/shard_map/ppermute | solution.py:79
  195.4 2.5 collective-permute-start.5
  197.9 6.0 %collective-permute-done.5 = f32[2,64,256]{2,1,0:T(8,128)S(1)} collective-permute-done((f32[2,64,256]{2,1,0:T(8,128)S(1)}, f32[2,64,256]{2,1,0:T(8,128)S(1)}, u32[]{:S(2)}, u32[]{:S(2)}) %collective-permute-start.5) | collective-permute-done | bytes 131104 | tf_op jit(solution)/shard_map/ppermute | solution.py:79
  203.9 0.6 fusion.26
  204.5 0.0 all-reduce.11.cloned.1.call-update
  204.5 42.0 %all-reduce.11.cloned.1.call-done = f32[1,64,256]{2,1,0:T(8,128)} async-done(((f32[1,64,256]{2,1,0:T(8,128)}), f32[1,64,256]{2,1,0:T(8,128)}) %all-reduce.11.cloned.1.call-update) | async-done | bytes 65552 | tf_op jit(solution)/shard_map/psum | solution.py:9
  246.5 1.0 convolution_bitcast_fusion
  247.5 0.7 pad_maximum_fusion
  (12 shorter events, 0.1 us)
Async XLA Ops:
  6.5 18.4 %copy-start.1 = (bf16[2,1,2,256,256]{4,3,2,1,0:T(8,128)(2,1)S(1)}, bf16[2,1,2,256,256]{4,3,2,1,0:T(8,128)(2,1)}, u32[]{:S(2)}) copy-start(bf16[2,1,2,256,256]{4,3,2,1,0:T(8,128)(2,1)} %param.10) | copy-start | bytes 1572868
  6.5 62.3 %all-reduce.5.cloned.1.call-start = ((), (), s32[]{:S(2)}) async-start(), calls=%async_computation | async-start | bytes 131072 | tf_op jit(solution)/shard_map/psum | solution.py:52
  24.3 44.5 %copy-start = (bf16[3,1,256,256]{3,2,1,0:T(8,128)(2,1)S(1)}, bf16[3,1,256,256]{3,2,1,0:T(8,128)(2,1)}, u32[]{:S(2)}) copy-start(bf16[3,1,256,256]{3,2,1,0:T(8,128)(2,1)} %param.9) | copy-start | bytes 1179652
  24.9 43.9 %copy-start.2 = (bf16[3,1,64,256]{3,2,1,0:T(8,128)(2,1)S(1)}, bf16[3,1,64,256]{3,2,1,0:T(8,128)(2,1)}, u32[]{:S(2)}) copy-start(bf16[3,1,64,256]{3,2,1,0:T(8,128)(2,1)} %param.8) | copy-start | bytes 294916
  25.8 101.7 %all-reduce.7.cloned.1.call-start = ((), (), s32[]{:S(2)}) async-start(), calls=%async_computation.1 | async-start | bytes 131072 | tf_op jit(solution)/shard_map/psum | solution.py:52
  85.5 101.5 %all-reduce.9.cloned.1.call-start = ((), (), s32[]{:S(2)}) async-start(), calls=%async_computation.2 | async-start | bytes 131072 | tf_op jit(solution)/shard_map/psum | solution.py:9
  128.9 1.4 collective-permute-start
  130.3 5.6 %collective-permute-start.1 = (f32[2,64,256]{2,1,0:T(8,128)S(1)}, f32[2,64,256]{2,1,0:T(8,128)S(1)}, u32[]{:S(2)}, u32[]{:S(2)}) collective-permute-start(f32[2,64,256]{2,1,0:T(8,128)S(1)} %add.70), channel_id=1, source_target_pairs={{0,8},{4,12},{8,0},{12,4},{16,24},{20,28},{24,16},{28,20},{1,9},{5... | collective-permute-start | bytes 393224 | tf_op jit(solution)/shard_map/ppermute | solution.py:79
  136.0 8.5 %collective-permute-start.2 = (f32[2,64,256]{2,1,0:T(8,128)S(1)}, f32[2,64,256]{2,1,0:T(8,128)S(1)}, u32[]{:S(2)}, u32[]{:S(2)}) collective-permute-start(f32[2,64,256]{2,1,0:T(8,128)S(1)} %add.71), channel_id=1, source_target_pairs={{0,16},{4,20},{8,24},{12,28},{16,0},{20,4},{24,8},{28,12},{1,17},{... | collective-permute-start | bytes 393224 | tf_op jit(solution)/shard_map/ppermute | solution.py:79
  145.1 101.4 %all-reduce.11.cloned.1.call-start = ((), (), s32[]{:S(2)}) async-start(), calls=%async_computation.3 | async-start | bytes 131072 | tf_op jit(solution)/shard_map/psum | solution.py:9
  188.3 1.4 collective-permute-start.3
  189.8 5.6 %collective-permute-start.4 = (f32[2,64,256]{2,1,0:T(8,128)S(1)}, f32[2,64,256]{2,1,0:T(8,128)S(1)}, u32[]{:S(2)}, u32[]{:S(2)}) collective-permute-start(f32[2,64,256]{2,1,0:T(8,128)S(1)} %add.74), channel_id=1, source_target_pairs={{0,8},{4,12},{8,0},{12,4},{16,24},{20,28},{24,16},{28,20},{1,9},{5... | collective-permute-start | bytes 393224 | tf_op jit(solution)/shard_map/ppermute | solution.py:79
  195.4 8.5 %collective-permute-start.5 = (f32[2,64,256]{2,1,0:T(8,128)S(1)}, f32[2,64,256]{2,1,0:T(8,128)S(1)}, u32[]{:S(2)}, u32[]{:S(2)}) collective-permute-start(f32[2,64,256]{2,1,0:T(8,128)S(1)} %add.75), channel_id=1, source_target_pairs={{0,16},{4,20},{8,24},{12,28},{16,0},{20,4},{24,8},{28,12},{1,17},{... | collective-permute-start | bytes 393224 | tf_op jit(solution)/shard_map/ppermute | solution.py:79
Sparse Core Ops, SparseCore 0:
  25.9 42.8 all-reduce.4
  85.6 41.7 all-reduce.6
  145.2 41.7 all-reduce.8
  204.6 41.8 all-reduce.10
